TPU v7x, 32 devices: a whole 2x2x4 slice. The times are simulated.
32 devices in a mesh: dp: 4 (over z), vocab: 8 (over y, x, core).
Axes of the slice: x: 2, y: 2, z: 4, core: 2. Of those that a mesh axis runs over, the one named last changes fastest.
Arguments:
- hidden: bfloat16 [4096, 4096], P(('dp', 'vocab')), may hold values from -4 to 4
- output_weight: bfloat16 [4096, 8192], P(None, 'vocab'), may hold values from -0.09375 to 0.09375
- owners: int32 [4096, 3], P(('dp', 'vocab')), may hold values from 0 to 7, all different within a row; in each aligned block of 128 rows (0 to 127, 128 to 255, ...) at most 64 rows name the same one
- negatives: int32 [4096, 3, 2], P(('dp', 'vocab')), may hold values from 0 to 7
- negative_mask: int32 [4096, 3, 2], P(('dp', 'vocab')), may hold values 0 or 1
- target_block: int32 [4096], P(('dp', 'vocab')), may hold values from 0 to 7
- target_word: int32 [4096], P(('dp', 'vocab')), may hold values from 0 to 127
- log_norm: bfloat16 [4096], P(('dp', 'vocab')), may hold values from 1 to 2
- cotangent: bfloat16 [4096], P(('dp', 'vocab')), may hold values from 4 to 8
Outputs:
- hidden_grad: bfloat16 [4096, 4096], P(('dp', 'vocab'))
- weight_grad: bfloat16 [4096, 8192], P('dp', 'vocab')
Inputs may be any that keep to these rules, and one draw needn't show every extreme that they name: Each row names 3 different owners; among the 128 rows of one device no owner is named by more than 64 rows, and in some device's rows an owner is named by exactly 64.
All inputs are finite; a program needn't handle non-finite values. No bound on the sum of `negative_mask` on one device may be relied on, other than what follows from the above.
Results may differ from a plain program's by a relative error of at most 0.015.
Values may be sent and summed in bfloat16 or wider, within the bound.
A program may use at most 128 MiB of HBM per device.

v0:
```python
import jax
import jax.numpy as jnp
from jax import lax
from jax.sharding import PartitionSpec as P

BLOCK = 128
BLK_DEV = 8
F32 = jnp.float32
BF16 = jnp.bfloat16


def body(
    hidden,
    output_weight,
    owners,
    negatives,
    negative_mask,
    target_block,
    target_word,
    log_norm,
    cotangent,
):
    tokens, width = hidden.shape
    visits = owners.shape[1]
    per_own = negatives.shape[2]
    n_vocab = lax.axis_size("vocab")
    n_dp = lax.axis_size("dp")
    me = lax.axis_index("vocab")
    my_dp = lax.axis_index("dp")
    words = output_weight.shape[1]
    capacity = max(2, tokens * visits * 4 // (3 * n_vocab))
    slots = n_vocab * capacity
    part = width // n_dp
    facts = jnp.concatenate(
        [
            owners.T,
            negatives.reshape(tokens, -1).T,
            negative_mask.reshape(tokens, -1).T,
            target_block[None, :],
            target_word[None, :],
        ],
        axis=0,
    ).astype(BF16)
    facts = jnp.concatenate([facts, log_norm[None, :], cotangent[None, :]], axis=0)
    facts = lax.all_gather(facts, ("dp", "vocab"), axis=0, tiled=False)
    blocks = n_dp * n_vocab
    group_rows = lax.all_gather(hidden, "vocab", axis=0, tiled=False)
    part_rows = lax.all_to_all(hidden, "dp", split_axis=1, concat_axis=0, tiled=True)
    part_rows = lax.all_gather(part_rows.reshape(n_dp, tokens, part), "vocab", axis=1)
    f = facts.astype(F32)
    pairs = visits * per_own
    hit = f[:, :visits, :] == me.astype(F32)
    neg = f[:, visits : visits + pairs, :]
    mask = f[:, visits + pairs : visits + 2 * pairs, :]
    base = visits + 2 * pairs
    t_block, t_word, norm, cot = (f[:, base + i, :] for i in range(4))
    named = jnp.any(hit, axis=1)
    cand = [jnp.where(hit[:, 0], t_block + 1.0, 0.0)]
    for n in range(per_own):
        value = jnp.zeros_like(t_block)
        for v in range(visits):
            i = v * per_own + n
            value = jnp.where(hit[:, v] & (mask[:, i] == 1.0), neg[:, i] + 1.0, value)
        cand.append(value)
    only = []
    for k, value in enumerate(cand):
        for earlier in cand[:k]:
            value = jnp.where(value == earlier, 0.0, value)
        only.append(value)
    upper = jnp.triu(jnp.ones((tokens, tokens), BF16), 1)
    rank = jnp.dot(named.astype(BF16), upper, preferred_element_type=F32)
    place = jnp.where(named, rank, -1.0)
    pick = (
        place[:, None, :] == jnp.arange(capacity, dtype=jnp.int32).astype(F32)[None, :, None]
    ).astype(BF16)
    attrs = jnp.stack(cand + only + [t_word, norm, cot], axis=1).astype(BF16)
    slot_facts = jnp.einsum("sct,sat->sca", pick, attrs, preferred_element_type=F32)
    kinds = per_own + 1
    all_only = slot_facts[:, :, kinds : 2 * kinds].reshape(n_dp * slots, kinds)
    mine = lax.dynamic_slice_in_dim(slot_facts, my_dp * n_vocab, n_vocab, 0).reshape(slots, -1)
    my_pick = lax.dynamic_slice_in_dim(pick, my_dp * n_vocab, n_vocab, 0)
    rows = jnp.einsum("sct,sth->sch", my_pick, group_rows, preferred_element_type=F32)
    rows = rows.astype(BF16).reshape(slots, width)
    scores = jnp.dot(rows, output_weight, preferred_element_type=F32)
    word_ids = jnp.arange(words, dtype=jnp.int32)[None, :]
    word_block = (word_ids // BLOCK + 1).astype(F32)
    word_in = (word_ids % BLOCK).astype(F32)
    counts = jnp.zeros((slots, words), F32)
    for k in range(kinds):
        counts = counts + jnp.where(mine[:, k : k + 1] == word_block, 1.0, 0.0)
    hot = jnp.where(
        (mine[:, 0:1] == word_block) & (mine[:, 2 * kinds : 2 * kinds + 1] == word_in), 1.0, 0.0
    )
    norm_col = mine[:, 2 * kinds + 1 : 2 * kinds + 2]
    cot_col = mine[:, 2 * kinds + 2 : 2 * kinds + 3]
    grown = jnp.where(counts > 0.0, counts * jnp.exp(scores - norm_col), 0.0)
    grad = (cot_col * (grown - hot)).astype(BF16)
    packed = []
    for k in range(kinds):
        which = mine[:, kinds + k : kinds + k + 1]
        value = jnp.zeros((slots, BLOCK), BF16)
        for b in range(BLK_DEV):
            value = jnp.where(which == b + 1.0, grad[:, b * BLOCK : (b + 1) * BLOCK], value)
        packed.append(value)
    packed = jnp.concatenate(packed, axis=1)
    packed = lax.all_gather(packed, "dp", axis=0, tiled=True)
    back = lax.dot_general(
        grad, output_weight, (((1,), (1,)), ((), ())), preferred_element_type=F32
    ).astype(BF16)
    back = jnp.einsum(
        "sct,sch->sth", my_pick, back.reshape(n_vocab, capacity, width), preferred_element_type=F32
    ).astype(BF16)
    hidden_grad = lax.psum_scatter(
        back.reshape(n_vocab * tokens, width), "vocab", scatter_dimension=0, tiled=True
    )
    part_slots = (
        jnp.einsum(
            "sct,sth->sch",
            pick,
            part_rows.reshape(blocks, tokens, part),
            preferred_element_type=F32,
        )
        .astype(BF16)
        .reshape(n_dp * slots, part)
    )
    spread = []
    for b in range(BLK_DEV):
        value = jnp.zeros((n_dp * slots, BLOCK), BF16)
        for k in range(kinds):
            value = jnp.where(
                all_only[:, k : k + 1] == b + 1.0, packed[:, k * BLOCK : (k + 1) * BLOCK], value
            )
        spread.append(value)
    spread = jnp.concatenate(spread, axis=1)
    weight_grad = lax.dot_general(
        part_slots, spread, (((0,), (0,)), ((), ())), preferred_element_type=F32
    ).astype(BF16)
    return (hidden_grad, weight_grad)


def solution(mesh):
    placed = (
        P(("dp", "vocab"), None),
        P(None, "vocab"),
        P(("dp", "vocab"), None),
        P(("dp", "vocab"), None, None),
        P(("dp", "vocab"), None, None),
        P(("dp", "vocab")),
        P(("dp", "vocab")),
        P(("dp", "vocab")),
        P(("dp", "vocab")),
    )
    return jax.shard_map(
        body,
        mesh=mesh,
        in_specs=placed,
        out_specs=(P(("dp", "vocab"), None), P("dp", "vocab")),
        check_vma=False,
    )
```

profile of v0, /device:TPU:0, one launch (start us, length us, event | category | flops | bytes accessed | tf_op | source)
XLA Modules:
  0.0 244.4 jit_solution(17321458530008942813)
XLA Ops:
  7.2 0.0 copy-start.2
  7.2 0.0 copy-start.3
  7.2 0.0 copy-start.5
  7.2 0.0 copy-start.6
  7.2 0.0 copy-start.4
  7.2 0.0 copy-start.7
  7.2 0.0 copy-start.8
  7.2 0.0 all-gather.10.cloned.1.call-start
  7.3 0.7 all-gather.10.cloned.1.call-update
  8.0 0.0 all-gather.12.cloned.1.call-start
  8.0 1.3 copy.20
  9.3 32.0 %all_to_all.16 = bf16[128,4,1024]{2,0,1:T(8,128)(2,1)} all-to-all(bf16[128,4,1024]{2,0,1:T(8,128)(2,1)S(1)} %bitcast.55), channel_id=1, replica_groups=mesh['dp'=4,'vocab'=8] {'dp'}, dimensions={1} | all-to-all | bytes 2097152 | tf_op jit(solution)/shard_map/all_to_all | solution.py:48
  41.3 0.0 all-gather.12.cloned.1.call-update
  41.3 0.0 all-gather.8.cloned.1.call-start
  41.4 0.0 copy-done.2
  41.4 0.0 copy-done.3
  41.5 0.0 copy-done.5
  41.5 0.0 copy-done.6
  41.5 0.0 copy-done.4
  41.5 0.0 copy-done.7
  41.5 0.0 copy-done.8
  41.5 0.2 concatenate.12
  41.7 40.7 %all-gather.3 = bf16[32,19,128]{2,1,0:T(8,128)(2,1)S(1)} all-gather(bf16[1,19,128]{2,1,0:T(8,128)(2,1)S(1)} %bitcast.56), channel_id=2, replica_groups=mesh['dp'=4,'vocab'=8] {'dp','vocab'}, dimensions={0}, use_global_device_ids=true | all-gather | bytes 160512 | tf_op jit(solution)/shard_map/all_gather | solution.py:45
  82.4 0.1 fusion.33
  82.5 0.3 fusion.17
  82.9 0.4 stack.4
  83.3 0.1 convolution_select_fusion
  83.4 0.5 fusion.3
  83.9 0.1 reshape.102
  84.0 0.1 compare_reduce_fusion.47
  84.2 0.2 broadcast_compare_fusion
  84.4 0.0 all-gather.10.cloned.1.call-done
  84.4 4.6 %convolution_convert_fusion.2 = bf16[8,64,4096]{2,1,0:T(8,128)(2,1)S(1)} fusion(bf16[8,128,4096]{2,1,0:T(8,128)(2,1)} %bitcast.48, pred[32,64,128]{2,1,0:T(32,128)(4,1)S(1)} %broadcast_compare_fusion, s32[]{:T(128)S(6)} %select_n.256), kind=kOutput, calls=%fused_computation.2 | convolution fusion | flops 538968064 | bytes 12648452 | tf_op jit(solution)/shard_map/sct,sth->sch/dot_general | solution.py:82
  89.1 8.7 %multiply_convert_fusion = bf16[512,1024]{1,0:T(8,128)(2,1)S(1)} fusion(bf16[512,4096]{1,0:T(8,128)(2,1)S(1)} %bitcast.49, bf16[4096,1024]{1,0:T(8,128)(2,1)} %param.10, f32[1024]{0:T(1024)S(1)} %get-tuple-element.78, f32[512]{0:T(512)S(1)} %bitcast.61, f32[1024]{0:T(1024)S(1)} %get-tuple-element.77, f32[512]{0:T(512)S(1)} %bitcast.64, f32[512]{0:T(512)S(1)} %bitcast.60, ...), kind=kOutput, calls=%fused_computation.8 | convolution fusion | flops 4304404480 | bytes 13651968 | tf_op jit(solution)/shard_map/dot_general | solution.py:84
  97.8 0.8 select_select_fusion
  98.5 0.8 select_select_fusion.1
  99.3 0.8 select_select_fusion.2
  100.1 0.8 pad_maximum_fusion
  100.9 0.0 all-gather.8.cloned.1.call-update
  100.9 0.2 reduce-scatter.2.cloned.1.call-start
  101.1 8.2 %convolution_convert_fusion.1 = bf16[512,4096]{1,0:T(8,128)(2,1)S(1)} fusion(bf16[512,1024]{1,0:T(8,128)(2,1)S(1)} %multiply_convert_fusion, bf16[4096,1024]{1,0:T(8,128)(2,1)} %param.10), kind=kOutput, calls=%fused_computation.1 | convolution fusion | flops 4297064448 | bytes 13631488 | tf_op jit(solution)/shard_map/dot_general | solution.py:107
  109.3 5.6 %convolution_convert_fusion = bf16[8,128,4096]{2,1,0:T(8,128)(2,1)} fusion(bf16[8,64,4096]{2,1,0:T(8,128)(2,1)S(1)} %bitcast.52, pred[32,64,128]{2,1,0:T(32,128)(4,1)S(1)} %broadcast_compare_fusion, s32[]{:T(128)S(6)} %select_n.256), kind=kOutput, calls=%fused_computation | convolution fusion | flops 541065216 | bytes 12648452 | tf_op jit(solution)/shard_map/sct,sch->sth/dot_general | solution.py:110
  114.9 0.0 reduce-scatter.2.cloned.1.call-update
  115.0 0.1 reshape.108
  115.1 0.6 compare_reduce_fusion.2
  115.7 8.7 %all-gather.12.cloned.1.call-done = bf16[4,1024,1024]{2,1,0:T(8,128)(2,1)} async-done(((bf16[4,128,1024]{2,1,0:T(8,128)(2,1)}), bf16[4,1024,1024]{2,1,0:T(8,128)(2,1)}) %all-gather.12.cloned.1.call-update) | async-done | bytes 8388624 | tf_op jit(solution)/shard_map/all_gather | solution.py:49
  124.4 6.6 %convolution_convert_fusion.3 = bf16[32,64,1024]{2,1,0:T(8,128)(2,1)} fusion(bf16[32,128,1024]{2,1,0:T(8,128)(2,1)} %bitcast.50, f32[32,128]{1,0:T(8,128)S(1)} %convolution_select_fusion, f32[64]{0:T(128)S(1)} %iota_convert_fusion), kind=kOutput, calls=%fused_computation.3 | convolution fusion | flops 539230208 | bytes 12599552 | tf_op jit(solution)/shard_map/sct,sth->sch/dot_general | solution.py:117
  131.0 32.6 %all-gather.8.cloned.1.call-done = bf16[2048,384]{1,0:T(8,128)(2,1)} async-done(((bf16[512,384]{1,0:T(8,128)(2,1)}), bf16[2048,384]{1,0:T(8,128)(2,1)}) %all-gather.8.cloned.1.call-update) | async-done | bytes 1572880 | tf_op jit(solution)/shard_map/all_gather | solution.py:106
  163.6 0.0 copy-start
  163.6 3.5 %select_dynamic-update-slice_fusion.7 = bf16[2048,1024]{1,0:T(8,128)(2,1)S(1)} fusion(pred[2048]{0:T(1024)(128)(4,1)S(1)} %get-tuple-element.58, pred[2048]{0:T(1024)(128)(4,1)S(1)} %get-tuple-element.57, pred[2048]{0:T(1024)(128)(4,1)S(1)} %get-tuple-element.56, bf16[2048,384]{1,0:T(8,128)(2,1)} %all-gather.8.cloned.1.call-done), kind=kLoop, calls=%fused_computation.22 | loop fusion | flops 786431 | bytes 2103296
  167.1 3.4 %select_dynamic-update-slice_fusion.6 = bf16[2048,1024]{1,0:T(8,128)(2,1)S(1)} fusion(bf16[2048,1024]{1,0:T(8,128)(2,1)S(1)} %select_dynamic-update-slice_fusion.7, pred[2048]{0:T(1024)(128)(4,1)S(1)} %get-tuple-element.16, pred[2048]{0:T(1024)(128)(4,1)S(1)} %get-tuple-element.9, pred[2048]{0:T(1024)(128)(4,1)S(1)} %get-tuple-element.3, ...), kind=kLoop, calls=%fused_computation.21 | loop fusion | flops 786432 | bytes 2103296
  170.5 0.0 copy-done
  170.5 1.8 select_dynamic-update-slice_fusion.5
  172.3 1.8 select_dynamic-update-slice_fusion.4
  174.1 0.0 copy-start.1
  174.1 1.8 select_dynamic-update-slice_fusion.3
  175.9 1.8 select_dynamic-update-slice_fusion.2
  177.6 1.8 select_dynamic-update-slice_fusion.1
  179.4 1.8 select_dynamic-update-slice_fusion
  181.2 0.0 copy-done.1
  181.2 5.7 %convolution_convert_fusion.4 = bf16[1024,1024]{1,0:T(8,128)(2,1)} fusion(bf16[2048,1024]{1,0:T(8,128)(2,1)S(1)} %bitcast.51, bf16[2048,1024]{1,0:T(8,128)(2,1)S(1)} %select_dynamic-update-slice_fusion), kind=kOutput, calls=%fused_computation.9 | convolution fusion | flops 4296015872 | bytes 10485760 | tf_op jit(solution)/shard_map/dot_general | solution.py:135
  187.0 50.9 %reduce-scatter.2.cloned.1.call-done = bf16[128,4096]{1,0:T(8,128)(2,1)} async-done(((bf16[1024,4096]{1,0:T(8,128)(2,1)}), bf16[128,4096]{1,0:T(8,128)(2,1)}) %reduce-scatter.2.cloned.1.call-update) | async-done | bytes 1048592 | tf_op jit(solution)/shard_map/reduce_scatter | solution.py:113
  (16 shorter events, 0.2 us)
Async XLA Ops:
  7.2 34.2 %copy-start.2 = (s32[128,3,2]{0,2,1:T(2,128)S(1)}, s32[128,3,2]{0,2,1:T(2,128)}, u32[]{:S(2)}) copy-start(s32[128,3,2]{0,2,1:T(2,128)} %param.12) | copy-start | bytes 9220
  7.2 34.3 %copy-start.3 = (s32[128,3,2]{0,2,1:T(2,128)S(1)}, s32[128,3,2]{0,2,1:T(2,128)}, u32[]{:S(2)}) copy-start(s32[128,3,2]{0,2,1:T(2,128)} %param.13) | copy-start | bytes 9220
  7.2 34.3 %copy-start.5 = (s32[128]{0:T(128)S(1)}, s32[128]{0:T(128)}, u32[]{:S(2)}) copy-start(s32[128]{0:T(128)} %param.15) | copy-start | bytes 1540
  7.2 34.3 %copy-start.6 = (s32[128]{0:T(128)S(1)}, s32[128]{0:T(128)}, u32[]{:S(2)}) copy-start(s32[128]{0:T(128)} %param.14) | copy-start | bytes 1540
  7.2 34.3 %copy-start.4 = (s32[128,3]{0,1:T(4,128)S(1)}, s32[128,3]{0,1:T(4,128)}, u32[]{:S(2)}) copy-start(s32[128,3]{0,1:T(4,128)} %param.11) | copy-start | bytes 4612
  7.2 34.3 %copy-start.7 = (bf16[128]{0:T(256)(128)(2,1)S(1)}, bf16[128]{0:T(256)(128)(2,1)}, u32[]{:S(2)}) copy-start(bf16[128]{0:T(256)(128)(2,1)} %param.16) | copy-start | bytes 772
  7.2 34.3 %copy-start.8 = (bf16[128]{0:T(256)(128)(2,1)S(1)}, bf16[128]{0:T(256)(128)(2,1)}, u32[]{:S(2)}) copy-start(bf16[128]{0:T(256)(128)(2,1)} %param.17) | copy-start | bytes 772
  7.2 77.2 %all-gather.10.cloned.1.call-start = ((), (), s32[]{:S(2)}) async-start(), calls=%async_computation.4 | async-start | bytes 9437184 | tf_op jit(solution)/shard_map/all_gather | solution.py:47
  8.0 116.4 %all-gather.12.cloned.1.call-start = ((), (), s32[]{:S(2)}) async-start(), calls=%async_computation.5 | async-start | bytes 9437184 | tf_op jit(solution)/shard_map/all_gather | solution.py:49
  41.3 122.3 %all-gather.8.cloned.1.call-start = ((), (), s32[]{:S(2)}) async-start(), calls=%async_computation.3 | async-start | bytes 1966080 | tf_op jit(solution)/shard_map/all_gather | solution.py:106
  100.9 137.0 %reduce-scatter.2.cloned.1.call-start = ((), (), s32[]{:S(2)}) async-start(), calls=%async_computation.2 | async-start | bytes 9437184 | tf_op jit(solution)/shard_map/reduce_scatter | solution.py:113
  163.6 6.9 %copy-start = (bf16[2048,384]{1,0:T(8,128)(2,1)S(1)}, bf16[2048,384]{1,0:T(8,128)(2,1)}, u32[]{:S(2)}) copy-start(bf16[2048,384]{1,0:T(8,128)(2,1)} %all-gather.8.cloned.1.call-done) | copy-start | bytes 4718596
  174.1 7.1 %copy-start.1 = (bf16[32,64,1024]{2,1,0:T(8,128)(2,1)S(1)}, bf16[32,64,1024]{2,1,0:T(8,128)(2,1)}, u32[]{:S(2)}) copy-start(bf16[32,64,1024]{2,1,0:T(8,128)(2,1)} %convolution_convert_fusion.3) | copy-start | bytes 12582916
Sparse Core Ops, SparseCore 0:
  9.9 58.0 all-gather.9
  70.0 54.3 all-gather.11
  126.5 37.0 all-gather.7
  167.5 70.3 reduce-scatter.1
where the time goes:
time: 245 us; the launch traced here: 244 us
  waiting for transfers between devices  93 us (38%)
  blocking collectives  72.6 us (30%)
  matrix products  40 us (16%)
  other arithmetic  22 us (9%)
  between operations  14.2 us (6%)
    reduce_scatter x1, waiting for transfers between devices, body(): lax.psum_scatter(back.reshape(n_vocab * tokens, width), 'vocab', scatter_...  50.9 us
    all_gather x1, blocking collectives, body(): facts = lax.all_gather(facts, ('dp', 'vocab'), axis=0, tiled=False)  40.7 us
    all_gather x1, waiting for transfers between devices, body(): packed = lax.all_gather(packed, 'dp', axis=0, tiled=True)  32.6 us
    all_to_all x1, blocking collectives, body(): lax.all_to_all(hidden, 'dp', split_axis=1, concat_axis=0, tiled=True)  32 us
    unnamed x7, other arithmetic  15.7 us
    all_gather x1, waiting for transfers between devices, body(): lax.all_gather(part_rows.reshape(n_dp, tokens, part), 'vocab', axis=1)  8.72 us
    dot_general x1, matrix products, body(): scores = jnp.dot(rows, output_weight, preferred_element_type=F32)  8.7 us
    dot_general x1, matrix products, body(): lax.dot_general(grad, output_weight, (((1,), (1,)), ((), ())), preferred_...  8.19 us
  transfers between devices with their start and end apart: 4, of which 3 were waited for; matrix products, arithmetic and copies ran while one was open for 26% of the time, Pallas kernels for 0%

commit v1 on v0

--- a/solution.py
+++ b/solution.py
@@ -7,6 +7,18 @@
 BLK_DEV = 8
 F32 = jnp.float32
 BF16 = jnp.bfloat16
+
+
+def collect(array, axis, dim):
+    ways, here = (lax.axis_size(axis), lax.axis_index(axis))
+    grown, reach = (array, 1)
+    while reach < ways:
+        theirs = lax.ppermute(grown, axis, [(d, d ^ reach) for d in range(ways)])
+        mine_first = jnp.concatenate([grown, theirs], axis=dim)
+        theirs_first = jnp.concatenate([theirs, grown], axis=dim)
+        grown = jnp.where(here & reach == 0, mine_first, theirs_first)
+        reach = 2 * reach
+    return grown
 
 
 def body(
@@ -103,7 +115,7 @@
             value = jnp.where(which == b + 1.0, grad[:, b * BLOCK : (b + 1) * BLOCK], value)
         packed.append(value)
     packed = jnp.concatenate(packed, axis=1)
-    packed = lax.all_gather(packed, "dp", axis=0, tiled=True)
+    packed = collect(packed, "dp", 0)
     back = lax.dot_general(
         grad, output_weight, (((1,), (1,)), ((), ())), preferred_element_type=F32
     ).astype(BF16)

time: 245 us -> 207 us (0.84)
  waiting for transfers between devices: 93 us -> 54.6 us
  other arithmetic: 22 us -> 25.4 us
  matrix products: 40 us -> 37.3 us
    ppermute x0 -> x2, waiting for transfers between devices: none -> 47.4 us  [collect(): theirs = lax.ppermute(grown, axis, [(d, d ^ reach) for d in range(ways)])]
    reduce_scatter x1, waiting for transfers between devices: 50.9 us -> 6.41 us  [body(): lax.psum_scatter(back.reshape(n_vocab * tokens, width), 'vocab', scatter_...]
    all_gather x1 -> x0, waiting for transfers between devices: 32.6 us -> none  [body(): packed = lax.all_gather(packed, 'dp', axis=0, tiled=True)]
    all_gather x1, waiting for transfers between devices: 8.72 us -> 0.01 us  [body(): lax.all_gather(part_rows.reshape(n_dp, tokens, part), 'vocab', axis=1)]
    dot_general x1, matrix products: 8.19 us -> 4.8 us  [body(): lax.dot_general(grad, output_weight, (((1,), (1,)), ((), ())), preferred_...]
    unnamed x7 -> x8, other arithmetic: 15.7 us -> 18.2 us
  transfers between devices with their start and end apart: 4 -> 5, of which waited for: 3 -> 3; matrix products, arithmetic and copies ran while one was open for 26% -> 31% of each run, Pallas kernels for 0% -> 0%
where the time goes in v1:
time: 207 us; the launch traced here: 206 us
  blocking collectives  72.6 us (35%)
  waiting for transfers between devices  54.6 us (26%)
  matrix products  37.3 us (18%)
  other arithmetic  25.4 us (12%)
  between operations  14.1 us (7%)
  local copies, waits for them, and re-layouts  2.19 us (1%)
    ppermute x2, waiting for transfers between devices, collect(): theirs = lax.ppermute(grown, axis, [(d, d ^ reach) for d in range(ways)])  47.4 us
    all_gather x1, blocking collectives, body(): facts = lax.all_gather(facts, ('dp', 'vocab'), axis=0, tiled=False)  40.7 us
    all_to_all x1, blocking collectives, body(): lax.all_to_all(hidden, 'dp', split_axis=1, concat_axis=0, tiled=True)  32 us
    unnamed x8, other arithmetic  18.2 us
    dot_general x1, matrix products, body(): scores = jnp.dot(rows, output_weight, preferred_element_type=F32)  8.85 us
    dot_general x1, matrix products, body(): lax.dot_general(part_slots, spread, (((0,), (0,)), ((), ())), preferred_e...  8.01 us
    reduce_scatter x1, waiting for transfers between devices, body(): lax.psum_scatter(back.reshape(n_vocab * tokens, width), 'vocab', scatter_...  6.41 us
    dot_general x1, matrix products, body(): jnp.einsum('sct,sch->sth', my_pick, back.reshape(n_vocab, capacity, width...  5.59 us
  transfers between devices with their start and end apart: 5, of which 3 were waited for; matrix products, arithmetic and copies ran while one was open for 31% of the time, Pallas kernels for 0%

profile of v1, /device:TPU:0, one launch (start us, length us, event | category | flops | bytes accessed | tf_op | source)
XLA Modules:
  0.0 206.5 jit_solution(9491375771601144752)
XLA Ops:
  7.2 0.0 copy-start
  7.2 0.0 copy-start.1
  7.2 0.0 copy-start.3
  7.2 0.0 copy-start.4
  7.2 0.0 copy-start.2
  7.2 0.0 copy-start.5
  7.2 0.0 copy-start.6
  7.2 0.0 all-gather.7.cloned.1.call-start
  7.3 0.7 all-gather.7.cloned.1.call-update
  8.0 0.0 all-gather.9.cloned.1.call-start
  8.0 1.3 copy.20
  9.3 32.0 %all_to_all.16 = bf16[128,4,1024]{2,0,1:T(8,128)(2,1)} all-to-all(bf16[128,4,1024]{2,0,1:T(8,128)(2,1)S(1)} %bitcast.55), channel_id=1, replica_groups=mesh['dp'=4,'vocab'=8] {'dp'}, dimensions={1} | all-to-all | bytes 2097152 | tf_op jit(solution)/shard_map/all_to_all | solution.py:60
  41.3 0.0 all-gather.9.cloned.1.call-update
  41.3 0.0 reduce-scatter.2.cloned.1.call-start
  41.4 0.0 copy-done
  41.4 0.0 copy-done.1
  41.5 0.0 copy-done.3
  41.5 0.0 copy-done.4
  41.5 0.0 copy-done.2
  41.5 0.0 copy-done.5
  41.5 0.0 copy-done.6
  41.5 0.2 concatenate.24
  41.7 40.7 %all-gather.3 = bf16[32,19,128]{2,1,0:T(8,128)(2,1)S(1)} all-gather(bf16[1,19,128]{2,1,0:T(8,128)(2,1)S(1)} %bitcast.56), channel_id=2, replica_groups=mesh['dp'=4,'vocab'=8] {'dp','vocab'}, dimensions={0}, use_global_device_ids=true | all-gather | bytes 160512 | tf_op jit(solution)/shard_map/all_gather | solution.py:57
  82.4 0.1 fusion.33
  82.5 0.3 fusion.17
  82.9 0.4 stack.4
  83.3 0.1 convolution_select_fusion
  83.4 0.5 fusion.3
  83.9 0.1 reshape.102
  84.0 0.2 broadcast_compare_fusion
  84.2 0.0 all-gather.7.cloned.1.call-done
  84.3 0.0 slice-start
  84.3 4.8 %convolution_convert_fusion.2 = bf16[8,64,4096]{2,1,0:T(8,128)(2,1)S(1)} fusion(bf16[8,128,4096]{2,1,0:T(8,128)(2,1)} %bitcast.48, pred[32,64,128]{2,1,0:T(32,128)(4,1)S(1)} %broadcast_compare_fusion, s32[]{:T(128)S(6)} %select_n.272), kind=kOutput, calls=%fused_computation.2 | convolution fusion | flops 538968064 | bytes 12648452 | tf_op jit(solution)/shard_map/sct,sth->sch/dot_general | solution.py:94
  89.1 0.0 slice-start.1
  89.1 8.8 %multiply_convert_fusion = bf16[512,1024]{1,0:T(8,128)(2,1)S(1)} fusion(bf16[512,4096]{1,0:T(8,128)(2,1)S(1)} %bitcast.49, bf16[4096,1024]{1,0:T(8,128)(2,1)} %param.10, f32[1024]{0:T(1024)S(1)} %get-tuple-element.78, f32[512]{0:T(512)S(1)} %bitcast.61, f32[1024]{0:T(1024)S(1)} %get-tuple-element.77, f32[512]{0:T(512)S(1)} %bitcast.64, f32[512]{0:T(512)S(1)} %bitcast.60, ...), kind=kOutput, calls=%fused_computation.8 | convolution fusion | flops 4304404480 | bytes 13651968 | tf_op jit(solution)/shard_map/dot_general | solution.py:96
  97.9 0.0 slice-done
  97.9 0.0 slice-done.1
  98.0 4.8 %convolution_convert_fusion.1 = bf16[512,4096]{1,0:T(8,128)(2,1)S(1)} fusion(bf16[512,1024]{1,0:T(8,128)(2,1)S(1)} %multiply_convert_fusion, bf16[4096,1024]{1,0:T(8,128)(2,1)S(1)} %bitcast.68), kind=kOutput, calls=%fused_computation.1 | convolution fusion | flops 4297064448 | bytes 13631488 | tf_op jit(solution)/shard_map/dot_general | solution.py:119
  102.8 5.6 %convolution_convert_fusion = bf16[8,128,4096]{2,1,0:T(8,128)(2,1)} fusion(bf16[8,64,4096]{2,1,0:T(8,128)(2,1)S(1)} %bitcast.52, pred[32,64,128]{2,1,0:T(32,128)(4,1)S(1)} %broadcast_compare_fusion, s32[]{:T(128)S(6)} %select_n.272), kind=kOutput, calls=%fused_computation | convolution fusion | flops 541065216 | bytes 12648452 | tf_op jit(solution)/shard_map/sct,sch->sth/dot_general | solution.py:122
  108.4 0.0 reduce-scatter.2.cloned.1.call-update
  108.4 0.2 compare_reduce_fusion.47
  108.5 0.8 select_select_fusion
  109.3 0.8 select_select_fusion.1
  110.1 0.9 select_select_fusion.2
  111.0 0.1 pad_maximum_fusion
  111.1 0.1 collective-permute-start
  111.2 11.3 %collective-permute-done = bf16[512,384]{1,0:T(8,128)(2,1)S(1)} collective-permute-done((bf16[512,384]{1,0:T(8,128)(2,1)S(1)}, bf16[512,384]{1,0:T(8,128)(2,1)S(1)}, u32[]{:S(2)}, u32[]{:S(2)}) %collective-permute-start) | collective-permute-done | bytes 393248 | tf_op jit(solution)/shard_map/ppermute | solution.py:16
  122.5 0.3 maximum_select_fusion.1
  122.8 0.1 collective-permute-start.1
  122.9 0.1 reshape.108
  123.0 0.6 compare_reduce_fusion.2
  123.6 36.1 %collective-permute-done.1 = bf16[1024,384]{1,0:T(8,128)(2,1)S(1)} collective-permute-done((bf16[1024,384]{1,0:T(8,128)(2,1)S(1)}, bf16[1024,384]{1,0:T(8,128)(2,1)S(1)}, u32[]{:S(2)}, u32[]{:S(2)}) %collective-permute-start.1) | collective-permute-done | bytes 786464 | tf_op jit(solution)/shard_map/ppermute | solution.py:16
  159.7 0.4 maximum_select_fusion
  160.1 2.6 %select_dynamic-update-slice_fusion.7 = bf16[2048,1024]{1,0:T(8,128)(2,1)} fusion(pred[2048]{0:T(1024)(128)(4,1)S(1)} %get-tuple-element.58, pred[2048]{0:T(1024)(128)(4,1)S(1)} %get-tuple-element.57, pred[2048]{0:T(1024)(128)(4,1)S(1)} %get-tuple-element.56, bf16[2048,384]{1,0:T(8,128)(2,1)S(1)} %maximum_select_fusion), kind=kLoop, calls=%fused_computation.24 | loop fusion | flops 786431 | bytes 2103296
  162.7 2.6 %select_dynamic-update-slice_fusion.6 = bf16[2048,1024]{1,0:T(8,128)(2,1)} fusion(bf16[2048,1024]{1,0:T(8,128)(2,1)} %select_dynamic-update-slice_fusion.7, pred[2048]{0:T(1024)(128)(4,1)S(1)} %get-tuple-element.16, pred[2048]{0:T(1024)(128)(4,1)S(1)} %get-tuple-element.9, pred[2048]{0:T(1024)(128)(4,1)S(1)} %get-tuple-element.3, ...), kind=kLoop, calls=%fused_computation.23 | loop fusion | flops 786432 | bytes 2103296
  165.3 2.6 %select_dynamic-update-slice_fusion.5 = bf16[2048,1024]{1,0:T(8,128)(2,1)} fusion(bf16[2048,1024]{1,0:T(8,128)(2,1)} %select_dynamic-update-slice_fusion.6, pred[2048]{0:T(1024)(128)(4,1)S(1)} %get-tuple-element.17, pred[2048]{0:T(1024)(128)(4,1)S(1)} %get-tuple-element.10, pred[2048]{0:T(1024)(128)(4,1)S(1)} %get-tuple-element.4, ...), kind=kLoop, calls=%fused_computation.22 | loop fusion | flops 786432 | bytes 2103296
  167.9 2.6 %select_dynamic-update-slice_fusion.4 = bf16[2048,1024]{1,0:T(8,128)(2,1)} fusion(bf16[2048,1024]{1,0:T(8,128)(2,1)} %select_dynamic-update-slice_fusion.5, pred[2048]{0:T(1024)(128)(4,1)S(1)} %get-tuple-element.18, pred[2048]{0:T(1024)(128)(4,1)S(1)} %get-tuple-element.11, pred[2048]{0:T(1024)(128)(4,1)S(1)} %get-tuple-element.5, ...), kind=kLoop, calls=%fused_computation.21 | loop fusion | flops 786432 | bytes 2103296
  170.5 2.6 %select_dynamic-update-slice_fusion.3 = bf16[2048,1024]{1,0:T(8,128)(2,1)} fusion(bf16[2048,1024]{1,0:T(8,128)(2,1)} %select_dynamic-update-slice_fusion.4, pred[2048]{0:T(1024)(128)(4,1)S(1)} %get-tuple-element.19, pred[2048]{0:T(1024)(128)(4,1)S(1)} %get-tuple-element.12, pred[2048]{0:T(1024)(128)(4,1)S(1)} %get-tuple-element.6, ...), kind=kLoop, calls=%fused_computation.20 | loop fusion | flops 786432 | bytes 2103296
  173.1 2.6 %select_dynamic-update-slice_fusion.2 = bf16[2048,1024]{1,0:T(8,128)(2,1)} fusion(bf16[2048,1024]{1,0:T(8,128)(2,1)} %select_dynamic-update-slice_fusion.3, pred[2048]{0:T(1024)(128)(4,1)S(1)} %get-tuple-element.20, pred[2048]{0:T(1024)(128)(4,1)S(1)} %get-tuple-element.13, pred[2048]{0:T(1024)(128)(4,1)S(1)} %get-tuple-element.7, ...), kind=kLoop, calls=%fused_computation.19 | loop fusion | flops 786432 | bytes 2103296
  175.7 2.6 %select_dynamic-update-slice_fusion.1 = bf16[2048,1024]{1,0:T(8,128)(2,1)} fusion(bf16[2048,1024]{1,0:T(8,128)(2,1)} %select_dynamic-update-slice_fusion.2, pred[2048]{0:T(1024)(128)(4,1)S(1)} %get-tuple-element.59, pred[2048]{0:T(1024)(128)(4,1)S(1)} %get-tuple-element.14, pred[2048]{0:T(1024)(128)(4,1)S(1)} %get-tuple-element.8, ...), kind=kLoop, calls=%fused_computation.18 | loop fusion | flops 786432 | bytes 2103296
  178.3 2.6 %select_dynamic-update-slice_fusion = bf16[2048,1024]{1,0:T(8,128)(2,1)} fusion(bf16[2048,1024]{1,0:T(8,128)(2,1)} %select_dynamic-update-slice_fusion.1, pred[2048]{0:T(1024)(128)(4,1)S(1)} %get-tuple-element.60, pred[2048]{0:T(1024)(128)(4,1)S(1)} %get-tuple-element.15, pred[2048]{0:T(1024)(128)(4,1)S(1)} %get-tuple-element.2, ...), kind=kLoop, calls=%fused_computation.17 | loop fusion | flops 786432 | bytes 2103296 | tf_op jit(solution)/shard_map/concatenate | solution.py:146
  180.9 4.7 %convolution_convert_fusion.3 = bf16[32,64,1024]{2,1,0:T(8,128)(2,1)S(1)} fusion(bf16[32,128,1024]{2,1,0:T(8,128)(2,1)} %bitcast.50, f32[32,128]{1,0:T(8,128)S(1)} %convolution_select_fusion, f32[64]{0:T(128)S(1)} %iota_convert_fusion), kind=kOutput, calls=%fused_computation.3 | convolution fusion | flops 539230208 | bytes 12599552 | tf_op jit(solution)/shard_map/sct,sth->sch/dot_general | solution.py:129
  185.5 8.0 %convolution_convert_fusion.4 = bf16[1024,1024]{1,0:T(8,128)(2,1)} fusion(bf16[2048,1024]{1,0:T(8,128)(2,1)S(1)} %bitcast.51, bf16[2048,1024]{1,0:T(8,128)(2,1)} %select_dynamic-update-slice_fusion), kind=kOutput, calls=%fused_computation.9 | convolution fusion | flops 4296015872 | bytes 10485760 | tf_op jit(solution)/shard_map/dot_general | solution.py:147
  193.6 6.4 %reduce-scatter.2.cloned.1.call-done = bf16[128,4096]{1,0:T(8,128)(2,1)} async-done(((bf16[1024,4096]{1,0:T(8,128)(2,1)}), bf16[128,4096]{1,0:T(8,128)(2,1)}) %reduce-scatter.2.cloned.1.call-update) | async-done | bytes 1048592 | tf_op jit(solution)/shard_map/reduce_scatter | solution.py:125
  (18 shorter events, 0.2 us)
Async XLA Ops:
  7.2 34.2 %copy-start = (s32[128,3,2]{0,2,1:T(2,128)S(1)}, s32[128,3,2]{0,2,1:T(2,128)}, u32[]{:S(2)}) copy-start(s32[128,3,2]{0,2,1:T(2,128)} %param.12) | copy-start | bytes 9220
  7.2 34.3 %copy-start.1 = (s32[128,3,2]{0,2,1:T(2,128)S(1)}, s32[128,3,2]{0,2,1:T(2,128)}, u32[]{:S(2)}) copy-start(s32[128,3,2]{0,2,1:T(2,128)} %param.13) | copy-start | bytes 9220
  7.2 34.3 %copy-start.3 = (s32[128]{0:T(128)S(1)}, s32[128]{0:T(128)}, u32[]{:S(2)}) copy-start(s32[128]{0:T(128)} %param.15) | copy-start | bytes 1540
  7.2 34.3 %copy-start.4 = (s32[128]{0:T(128)S(1)}, s32[128]{0:T(128)}, u32[]{:S(2)}) copy-start(s32[128]{0:T(128)} %param.14) | copy-start | bytes 1540
  7.2 34.3 %copy-start.2 = (s32[128,3]{0,1:T(4,128)S(1)}, s32[128,3]{0,1:T(4,128)}, u32[]{:S(2)}) copy-start(s32[128,3]{0,1:T(4,128)} %param.11) | copy-start | bytes 4612
  7.2 34.3 %copy-start.5 = (bf16[128]{0:T(256)(128)(2,1)S(1)}, bf16[128]{0:T(256)(128)(2,1)}, u32[]{:S(2)}) copy-start(bf16[128]{0:T(256)(128)(2,1)} %param.16) | copy-start | bytes 772
  7.2 34.3 %copy-start.6 = (bf16[128]{0:T(256)(128)(2,1)S(1)}, bf16[128]{0:T(256)(128)(2,1)}, u32[]{:S(2)}) copy-start(bf16[128]{0:T(256)(128)(2,1)} %param.17) | copy-start | bytes 772
  7.2 77.0 %all-gather.7.cloned.1.call-start = ((), (), s32[]{:S(2)}) async-start(), calls=%async_computation.3 | async-start | bytes 9437184 | tf_op jit(solution)/shard_map/all_gather | solution.py:59
  8.0 172.9 %all-gather.9.cloned.1.call-start = ((), (), s32[]{:S(2)}) async-start(), calls=%async_computation.4 | async-start | bytes 9437184 | tf_op jit(solution)/shard_map/all_gather | solution.py:61
  41.3 158.6 %reduce-scatter.2.cloned.1.call-start = ((), (), s32[]{:S(2)}) async-start(), calls=%async_computation.2 | async-start | bytes 9437184 | tf_op jit(solution)/shard_map/reduce_scatter | solution.py:125
  84.3 13.7 %slice-start = ((s8[8388608]{0:T(1024)(128)(4,1)}), s8[4194304]{0:T(1024)(128)(4,1)S(1)}, s32[]{:S(2)}) async-start(s8[8388608]{0:T(1024)(128)(4,1)} %bitcast.67), calls=%async_computation.5 | async-start | bytes 8388608
  89.1 8.9 %slice-start.1 = ((s8[8388608]{0:T(1024)(128)(4,1)}), s8[4194304]{0:T(1024)(128)(4,1)S(1)}, s32[]{:S(2)}) async-start(s8[8388608]{0:T(1024)(128)(4,1)} %bitcast.67), calls=%async_computation.6 | async-start | bytes 8388608
  111.1 11.4 %collective-permute-start = (bf16[512,384]{1,0:T(8,128)(2,1)S(1)}, bf16[512,384]{1,0:T(8,128)(2,1)S(1)}, u32[]{:S(2)}, u32[]{:S(2)}) collective-permute-start(bf16[512,384]{1,0:T(8,128)(2,1)S(1)} %pad_maximum_fusion), channel_id=1, source_target_pairs={{0,8},{8,0},{16,24},{24,16},{1,9},{9,1},{17,25},{25,17},{2,10},{10... | collective-permute-start | bytes 1179656 | tf_op jit(solution)/shard_map/ppermute | solution.py:16
  122.8 36.9 %collective-permute-start.1 = (bf16[1024,384]{1,0:T(8,128)(2,1)S(1)}, bf16[1024,384]{1,0:T(8,128)(2,1)S(1)}, u32[]{:S(2)}, u32[]{:S(2)}) collective-permute-start(bf16[1024,384]{1,0:T(8,128)(2,1)S(1)} %maximum_select_fusion.1), channel_id=1, source_target_pairs={{0,16},{8,24},{16,0},{24,8},{1,17},{9,25},{17,1},{25,9},{2,18},{10... | collective-permute-start | bytes 2359304 | tf_op jit(solution)/shard_map/ppermute | solution.py:16
Sparse Core Ops, SparseCore 0:
  9.9 58.0 all-gather.6
  70.0 54.3 all-gather.8
  128.4 71.4 reduce-scatter.1
